TPU v7x, 128 devices: a whole 4x4x4 slice. The times are simulated.
128 devices in a mesh: section: 8 (over x, core), tp: 16 (over z, y).
Axes of the slice: x: 4, y: 4, z: 4, core: 2. Of those that a mesh axis runs over, the one named last changes fastest.
Arguments:
- layer_inputs: bfloat16 [16, 512, 4096], P('section', None, 'tp'), may hold values from -6 to 6
- weights: bfloat16 [16, 4096, 4096], P('section', 'tp'), may hold values from -0.046875 to 0.046875
- input_basis: bfloat16 [16, 4096, 64], P('section', 'tp'), may hold values from -0.09375 to 0.09375
- output_basis: bfloat16 [16, 4096, 32], P('section', 'tp'), may hold values from -0.09375 to 0.09375
- queries: bfloat16 [16, 512, 2048], P('section', 'tp'), may hold values from -0.00390625 to 0.00390625
- top_cotangent: bfloat16 [512, 4096], replicated, may hold values from -6 to 6
- sequence_example: int32 [4], replicated, may hold values from 0 to 1
Outputs:
- scores: float32 [2, 512], P(None, 'tp')
All inputs are finite; a program needn't handle non-finite values.
Results may differ from a plain program's by a relative error of at most 0.0094.
Values may be sent and summed in bfloat16 or wider, within the bound.
No kernel may reach another device: no remote copies, remote signals or barrier semaphores. Data moves between devices by JAX's collectives and lax.ppermute only.
A program may use at most 64 MiB of HBM per device.

v0:
```python
import jax
import jax.numpy as jnp
from jax import lax
from jax.sharding import PartitionSpec as P

SEQLEN = 128
SEQ_MB = 1
MB = 4
EXAMPLES = 2


def from_behind(value, axis, by):
    size = lax.axis_size(axis)
    pairs = [(i, i + by) for i in range(size) if 0 <= i + by < size]
    return lax.ppermute(value, axis, pairs)


def silu_parts(values):
    floats = values.astype(jnp.float32)
    logistic = jax.nn.sigmoid(floats)
    return ((floats * logistic).astype(jnp.bfloat16), logistic * (1.0 + floats * (1.0 - logistic)))


def contract_columns(portion, matrix):
    return lax.dot_general(
        portion, matrix, (((1,), (1,)), ((), ())), preferred_element_type=jnp.float32
    )


def outer_rows(out_feats, in_feats):
    joined = out_feats[:, :, :, None] * in_feats[:, :, None, :]
    return joined.reshape(joined.shape[0], joined.shape[1], -1)


def shards(
    layer_inputs, weights, input_basis, output_basis, queries, top_cotangent, sequence_example
):
    section_count = lax.axis_size("section")
    section_rank = lax.axis_index("section")
    tp_rank = lax.axis_index("tp")
    width_local = layer_inputs.shape[2]
    width_full = weights.shape[2]
    total_tokens = layer_inputs.shape[1]
    block_rows = SEQ_MB * SEQLEN
    activated, slopes = silu_parts(layer_inputs)
    partial_in = jnp.einsum(
        "ltd,ldr->tlr", activated, input_basis, preferred_element_type=jnp.float32
    )
    in_feats = lax.psum(partial_in.reshape(total_tokens, -1), "tp").reshape(partial_in.shape)
    example_index = jnp.arange(EXAMPLES, dtype=jnp.int32)
    is_top = section_rank == section_count - 1

    def fold_lower(portion):
        return contract_columns(portion, weights[0])

    def tick(tick_index, state):
        outgoing, grads, stored = state
        micro_index = tick_index - (section_count - 1 - section_rank)
        valid = (micro_index >= 0) & (micro_index < MB)
        micro_clip = jnp.clip(micro_index, 0, MB - 1)
        first_row = micro_clip * block_rows
        slope_block = lax.dynamic_slice_in_dim(slopes, first_row, block_rows, 1)
        received = from_behind(outgoing, "section", -1)
        top_block = lax.dynamic_slice_in_dim(top_cotangent, first_row, block_rows, 0)
        upper_full = jnp.where(is_top, top_block, received)
        upper_own = lax.dynamic_slice_in_dim(upper_full, tp_rank * width_local, width_local, 1)
        upper_branch = lax.dot_general(
            upper_full, weights[1], (((1,), (1,)), ((), ())), preferred_element_type=jnp.float32
        )
        middle_own = (upper_own.astype(jnp.float32) + slope_block[1] * upper_branch).astype(
            jnp.bfloat16
        )
        lower_branch = fold_lower(lax.all_gather(middle_own, "tp", axis=1, tiled=True))
        lower_own = (middle_own.astype(jnp.float32) + slope_block[0] * lower_branch).astype(
            jnp.bfloat16
        )
        new_outgoing = lax.all_gather(lower_own, "tp", axis=1, tiled=True)
        cotangents = jnp.stack([middle_own, upper_own], 0)
        partial_out = jnp.einsum(
            "lrd,ldk->rlk", cotangents, output_basis, preferred_element_type=jnp.float32
        )
        out_feats = lax.psum(partial_out.reshape(block_rows, -1), "tp").reshape(partial_out.shape)
        in_block = lax.dynamic_slice_in_dim(in_feats, first_row, block_rows, 0)
        block_examples = jnp.repeat(
            lax.dynamic_slice_in_dim(sequence_example, micro_clip * SEQ_MB, SEQ_MB, 0), SEQLEN
        )
        selector = (example_index[:, None] == block_examples[None, :]).astype(
            jnp.float32
        ) * valid.astype(jnp.float32)
        grads = grads + jnp.einsum(
            "er,rlk->lek",
            selector,
            outer_rows(out_feats, in_block),
            precision=lax.Precision.HIGHEST,
        )
        return (new_outgoing, grads, stored)

    outgoing_init = jnp.zeros((block_rows, width_full), jnp.bfloat16)
    grads_init = jnp.zeros((2, EXAMPLES, queries.shape[2]), jnp.float32)
    stored_init = jnp.zeros((1,), jnp.bfloat16)
    final_out, grads, stored = lax.fori_loop(
        0, MB + section_count - 1, tick, (outgoing_init, grads_init, stored_init)
    )
    layer_scores = jnp.einsum(
        "lek,lqk->eq", grads, queries.astype(jnp.float32), precision=lax.Precision.HIGHEST
    )
    return lax.psum(layer_scores, "section")


def solution(mesh):
    placed = (
        P("section", None, "tp"),
        P("section", "tp", None),
        P("section", "tp", None),
        P("section", "tp", None),
        P("section", "tp", None),
        P(),
        P(),
    )
    return jax.shard_map(
        shards, mesh=mesh, in_specs=placed, out_specs=P(None, "tp"), check_vma=False
    )
```

profile of v0, /device:TPU:1, one launch (start us, length us, event | category | flops | bytes accessed | tf_op | source)
XLA Modules:
  0.0 1662.4 jit_solution(13824720775074881913)
XLA Ops:
  9.2 87.7 %all-reduce.2.cloned.1.call-done = f32[512,2,64]{0,2,1:T(8,128)} async-done(((f32[512,2,64]{0,2,1:T(8,128)}), f32[512,2,64]{0,2,1:T(8,128)}) %all-reduce.2.cloned.1.call-update) | async-done | bytes 262160 | tf_op jit(solution)/shard_map/psum | solution.py:49
  98.0 1529.4 %while.18 = (s32[]{:T(128)}, bf16[128,4096]{1,0:T(8,128)(2,1)}, f32[2,2,2048]{2,1,0:T(2,128)S(1)}, pred[]{:T(512)}, s32[]{:T(128)}, /*index=5*/bf16[512,4096]{1,...) while((s32[]{:T(128)}, bf16[128,4096]{1,0:T(8,128)(2,1)}, ...), condition=%wide.region_3.4_spmd.clone, body=%wide.region_1.3_spmd.clone.sunk | while | flops 555048960 | bytes 25986044 | solution.py:101
  120.3 40.6 %all-gather.3.cloned.1.call-done = bf16[128,4096]{1,0:T(8,128)(2,1)} async-done(((bf16[128,256]{1,0:T(8,128)(2,1)}), bf16[128,4096]{1,0:T(8,128)(2,1)}) %all-gather.3.cloned.1.call-update) | async-done | bytes 1048592 | tf_op jit(solution)/shard_map/while/body/eval_jaxpr/all_gather | solution.py:73
  166.6 58.4 %psum.31 = f32[128,2,32]{0,2,1:T(8,128)S(1)} all-reduce(f32[128,2,32]{0,2,1:T(8,128)S(1)} %convolution_bitcast_fusion.5), channel_id=1, replica_groups=mesh['section'=8,'tp'=16] {'tp'}, use_global_device_ids=true, to_apply=%region_2.2 | all-reduce | flops 8192 | bytes 65536 | tf_op jit(solution)/shard_map/while/body/eval_jaxpr/psum | solution.py:82
  263.3 37.6 %all-gather.3.cloned.1.call-done = bf16[128,4096]{1,0:T(8,128)(2,1)} async-done(((bf16[128,256]{1,0:T(8,128)(2,1)}), bf16[128,4096]{1,0:T(8,128)(2,1)}) %all-gather.3.cloned.1.call-update) | async-done | bytes 1048592 | tf_op jit(solution)/shard_map/while/body/eval_jaxpr/all_gather | solution.py:73
  306.6 58.4 %psum.31 = f32[128,2,32]{0,2,1:T(8,128)S(1)} all-reduce(f32[128,2,32]{0,2,1:T(8,128)S(1)} %convolution_bitcast_fusion.5), channel_id=1, replica_groups=mesh['section'=8,'tp'=16] {'tp'}, use_global_device_ids=true, to_apply=%region_2.2 | all-reduce | flops 8192 | bytes 65536 | tf_op jit(solution)/shard_map/while/body/eval_jaxpr/psum | solution.py:82
  403.3 37.6 %all-gather.3.cloned.1.call-done = bf16[128,4096]{1,0:T(8,128)(2,1)} async-done(((bf16[128,256]{1,0:T(8,128)(2,1)}), bf16[128,4096]{1,0:T(8,128)(2,1)}) %all-gather.3.cloned.1.call-update) | async-done | bytes 1048592 | tf_op jit(solution)/shard_map/while/body/eval_jaxpr/all_gather | solution.py:73
  446.6 58.4 %psum.31 = f32[128,2,32]{0,2,1:T(8,128)S(1)} all-reduce(f32[128,2,32]{0,2,1:T(8,128)S(1)} %convolution_bitcast_fusion.5), channel_id=1, replica_groups=mesh['section'=8,'tp'=16] {'tp'}, use_global_device_ids=true, to_apply=%region_2.2 | all-reduce | flops 8192 | bytes 65536 | tf_op jit(solution)/shard_map/while/body/eval_jaxpr/psum | solution.py:82
  543.4 37.6 %all-gather.3.cloned.1.call-done = bf16[128,4096]{1,0:T(8,128)(2,1)} async-done(((bf16[128,256]{1,0:T(8,128)(2,1)}), bf16[128,4096]{1,0:T(8,128)(2,1)}) %all-gather.3.cloned.1.call-update) | async-done | bytes 1048592 | tf_op jit(solution)/shard_map/while/body/eval_jaxpr/all_gather | solution.py:73
  586.7 58.4 %psum.31 = f32[128,2,32]{0,2,1:T(8,128)S(1)} all-reduce(f32[128,2,32]{0,2,1:T(8,128)S(1)} %convolution_bitcast_fusion.5), channel_id=1, replica_groups=mesh['section'=8,'tp'=16] {'tp'}, use_global_device_ids=true, to_apply=%region_2.2 | all-reduce | flops 8192 | bytes 65536 | tf_op jit(solution)/shard_map/while/body/eval_jaxpr/psum | solution.py:82
  683.4 37.6 %all-gather.3.cloned.1.call-done = bf16[128,4096]{1,0:T(8,128)(2,1)} async-done(((bf16[128,256]{1,0:T(8,128)(2,1)}), bf16[128,4096]{1,0:T(8,128)(2,1)}) %all-gather.3.cloned.1.call-update) | async-done | bytes 1048592 | tf_op jit(solution)/shard_map/while/body/eval_jaxpr/all_gather | solution.py:73
  726.7 58.4 %psum.31 = f32[128,2,32]{0,2,1:T(8,128)S(1)} all-reduce(f32[128,2,32]{0,2,1:T(8,128)S(1)} %convolution_bitcast_fusion.5), channel_id=1, replica_groups=mesh['section'=8,'tp'=16] {'tp'}, use_global_device_ids=true, to_apply=%region_2.2 | all-reduce | flops 8192 | bytes 65536 | tf_op jit(solution)/shard_map/while/body/eval_jaxpr/psum | solution.py:82
  823.4 37.6 %all-gather.3.cloned.1.call-done = bf16[128,4096]{1,0:T(8,128)(2,1)} async-done(((bf16[128,256]{1,0:T(8,128)(2,1)}), bf16[128,4096]{1,0:T(8,128)(2,1)}) %all-gather.3.cloned.1.call-update) | async-done | bytes 1048592 | tf_op jit(solution)/shard_map/while/body/eval_jaxpr/all_gather | solution.py:73
  866.7 58.4 %psum.31 = f32[128,2,32]{0,2,1:T(8,128)S(1)} all-reduce(f32[128,2,32]{0,2,1:T(8,128)S(1)} %convolution_bitcast_fusion.5), channel_id=1, replica_groups=mesh['section'=8,'tp'=16] {'tp'}, use_global_device_ids=true, to_apply=%region_2.2 | all-reduce | flops 8192 | bytes 65536 | tf_op jit(solution)/shard_map/while/body/eval_jaxpr/psum | solution.py:82
  963.4 37.6 %all-gather.3.cloned.1.call-done = bf16[128,4096]{1,0:T(8,128)(2,1)} async-done(((bf16[128,256]{1,0:T(8,128)(2,1)}), bf16[128,4096]{1,0:T(8,128)(2,1)}) %all-gather.3.cloned.1.call-update) | async-done | bytes 1048592 | tf_op jit(solution)/shard_map/while/body/eval_jaxpr/all_gather | solution.py:73
  1006.7 58.4 %psum.31 = f32[128,2,32]{0,2,1:T(8,128)S(1)} all-reduce(f32[128,2,32]{0,2,1:T(8,128)S(1)} %convolution_bitcast_fusion.5), channel_id=1, replica_groups=mesh['section'=8,'tp'=16] {'tp'}, use_global_device_ids=true, to_apply=%region_2.2 | all-reduce | flops 8192 | bytes 65536 | tf_op jit(solution)/shard_map/while/body/eval_jaxpr/psum | solution.py:82
  1103.5 37.6 %all-gather.3.cloned.1.call-done = bf16[128,4096]{1,0:T(8,128)(2,1)} async-done(((bf16[128,256]{1,0:T(8,128)(2,1)}), bf16[128,4096]{1,0:T(8,128)(2,1)}) %all-gather.3.cloned.1.call-update) | async-done | bytes 1048592 | tf_op jit(solution)/shard_map/while/body/eval_jaxpr/all_gather | solution.py:73
  1146.8 58.4 %psum.31 = f32[128,2,32]{0,2,1:T(8,128)S(1)} all-reduce(f32[128,2,32]{0,2,1:T(8,128)S(1)} %convolution_bitcast_fusion.5), channel_id=1, replica_groups=mesh['section'=8,'tp'=16] {'tp'}, use_global_device_ids=true, to_apply=%region_2.2 | all-reduce | flops 8192 | bytes 65536 | tf_op jit(solution)/shard_map/while/body/eval_jaxpr/psum | solution.py:82
  1243.5 37.6 %all-gather.3.cloned.1.call-done = bf16[128,4096]{1,0:T(8,128)(2,1)} async-done(((bf16[128,256]{1,0:T(8,128)(2,1)}), bf16[128,4096]{1,0:T(8,128)(2,1)}) %all-gather.3.cloned.1.call-update) | async-done | bytes 1048592 | tf_op jit(solution)/shard_map/while/body/eval_jaxpr/all_gather | solution.py:73
  1286.8 58.4 %psum.31 = f32[128,2,32]{0,2,1:T(8,128)S(1)} all-reduce(f32[128,2,32]{0,2,1:T(8,128)S(1)} %convolution_bitcast_fusion.5), channel_id=1, replica_groups=mesh['section'=8,'tp'=16] {'tp'}, use_global_device_ids=true, to_apply=%region_2.2 | all-reduce | flops 8192 | bytes 65536 | tf_op jit(solution)/shard_map/while/body/eval_jaxpr/psum | solution.py:82
  1383.5 37.6 %all-gather.3.cloned.1.call-done = bf16[128,4096]{1,0:T(8,128)(2,1)} async-done(((bf16[128,256]{1,0:T(8,128)(2,1)}), bf16[128,4096]{1,0:T(8,128)(2,1)}) %all-gather.3.cloned.1.call-update) | async-done | bytes 1048592 | tf_op jit(solution)/shard_map/while/body/eval_jaxpr/all_gather | solution.py:73
  1426.8 58.4 %psum.31 = f32[128,2,32]{0,2,1:T(8,128)S(1)} all-reduce(f32[128,2,32]{0,2,1:T(8,128)S(1)} %convolution_bitcast_fusion.5), channel_id=1, replica_groups=mesh['section'=8,'tp'=16] {'tp'}, use_global_device_ids=true, to_apply=%region_2.2 | all-reduce | flops 8192 | bytes 65536 | tf_op jit(solution)/shard_map/while/body/eval_jaxpr/psum | solution.py:82
  1523.5 37.6 %all-gather.3.cloned.1.call-done = bf16[128,4096]{1,0:T(8,128)(2,1)} async-done(((bf16[128,256]{1,0:T(8,128)(2,1)}), bf16[128,4096]{1,0:T(8,128)(2,1)}) %all-gather.3.cloned.1.call-update) | async-done | bytes 1048592 | tf_op jit(solution)/shard_map/while/body/eval_jaxpr/all_gather | solution.py:73
  1566.8 58.4 %psum.31 = f32[128,2,32]{0,2,1:T(8,128)S(1)} all-reduce(f32[128,2,32]{0,2,1:T(8,128)S(1)} %convolution_bitcast_fusion.5), channel_id=1, replica_groups=mesh['section'=8,'tp'=16] {'tp'}, use_global_device_ids=true, to_apply=%region_2.2 | all-reduce | flops 8192 | bytes 65536 | tf_op jit(solution)/shard_map/while/body/eval_jaxpr/psum | solution.py:82
  (225 shorter events, 500.4 us)
Async XLA Ops:
  6.5 90.4 %all-reduce.2.cloned.1.call-start = ((), (), s32[]{:S(2)}) async-start(), calls=%async_computation | async-start | bytes 524288 | tf_op jit(solution)/shard_map/psum | solution.py:49
  98.0 62.9 %all-gather.3.cloned.1.call-start = ((), (), s32[]{:S(2)}) async-start(), calls=%async_computation.1 | async-start | bytes 1114112 | tf_op jit(solution)/shard_map/while/body/eval_jaxpr/all_gather | solution.py:73
  120.2 106.9 %all-gather.5.cloned.1.call-start = ((), (), s32[]{:S(2)}) async-start(), calls=%async_computation.2 | async-start | bytes 1114112 | tf_op jit(solution)/shard_map/while/body/eval_jaxpr/all_gather | solution.py:77
  227.2 73.7 %all-gather.3.cloned.1.call-start = ((), (), s32[]{:S(2)}) async-start(), calls=%async_computation.1 | async-start | bytes 1114112 | tf_op jit(solution)/shard_map/while/body/eval_jaxpr/all_gather | solution.py:73
  263.3 103.9 %all-gather.5.cloned.1.call-start = ((), (), s32[]{:S(2)}) async-start(), calls=%async_computation.2 | async-start | bytes 1114112 | tf_op jit(solution)/shard_map/while/body/eval_jaxpr/all_gather | solution.py:77
  367.2 73.8 %all-gather.3.cloned.1.call-start = ((), (), s32[]{:S(2)}) async-start(), calls=%async_computation.1 | async-start | bytes 1114112 | tf_op jit(solution)/shard_map/while/body/eval_jaxpr/all_gather | solution.py:73
  367.3 31.4 %collective-permute-start = (bf16[128,4096]{1,0:T(8,128)(2,1)}, bf16[128,4096]{1,0:T(8,128)(2,1)S(1)}, u32[]{:S(2)}, u32[]{:S(2)}) collective-permute-start(bf16[128,4096]{1,0:T(8,128)(2,1)} %get-tuple-element.465), channel_id=1, source_target_pairs={{16,0},{32,16},{48,32},{64,48},{80,64},{96,80},{112,96},{17,1},{33... | collective-permute-start | bytes 3145736 | tf_op jit(solution)/shard_map/while/body/eval_jaxpr/ppermute | solution.py:15
  403.3 103.9 %all-gather.5.cloned.1.call-start = ((), (), s32[]{:S(2)}) async-start(), calls=%async_computation.2 | async-start | bytes 1114112 | tf_op jit(solution)/shard_map/while/body/eval_jaxpr/all_gather | solution.py:77
  507.2 73.8 %all-gather.3.cloned.1.call-start = ((), (), s32[]{:S(2)}) async-start(), calls=%async_computation.1 | async-start | bytes 1114112 | tf_op jit(solution)/shard_map/while/body/eval_jaxpr/all_gather | solution.py:73
  543.3 103.9 %all-gather.5.cloned.1.call-start = ((), (), s32[]{:S(2)}) async-start(), calls=%async_computation.2 | async-start | bytes 1114112 | tf_op jit(solution)/shard_map/while/body/eval_jaxpr/all_gather | solution.py:77
  647.3 73.8 %all-gather.3.cloned.1.call-start = ((), (), s32[]{:S(2)}) async-start(), calls=%async_computation.1 | async-start | bytes 1114112 | tf_op jit(solution)/shard_map/while/body/eval_jaxpr/all_gather | solution.py:73
  683.3 103.9 %all-gather.5.cloned.1.call-start = ((), (), s32[]{:S(2)}) async-start(), calls=%async_computation.2 | async-start | bytes 1114112 | tf_op jit(solution)/shard_map/while/body/eval_jaxpr/all_gather | solution.py:77
  787.3 73.8 %all-gather.3.cloned.1.call-start = ((), (), s32[]{:S(2)}) async-start(), calls=%async_computation.1 | async-start | bytes 1114112 | tf_op jit(solution)/shard_map/while/body/eval_jaxpr/all_gather | solution.py:73
  823.4 103.9 %all-gather.5.cloned.1.call-start = ((), (), s32[]{:S(2)}) async-start(), calls=%async_computation.2 | async-start | bytes 1114112 | tf_op jit(solution)/shard_map/while/body/eval_jaxpr/all_gather | solution.py:77
  927.3 73.8 %all-gather.3.cloned.1.call-start = ((), (), s32[]{:S(2)}) async-start(), calls=%async_computation.1 | async-start | bytes 1114112 | tf_op jit(solution)/shard_map/while/body/eval_jaxpr/all_gather | solution.py:73
  963.4 103.9 %all-gather.5.cloned.1.call-start = ((), (), s32[]{:S(2)}) async-start(), calls=%async_computation.2 | async-start | bytes 1114112 | tf_op jit(solution)/shard_map/while/body/eval_jaxpr/all_gather | solution.py:77
  1067.3 73.8 %all-gather.3.cloned.1.call-start = ((), (), s32[]{:S(2)}) async-start(), calls=%async_computation.1 | async-start | bytes 1114112 | tf_op jit(solution)/shard_map/while/body/eval_jaxpr/all_gather | solution.py:73
  1103.4 103.9 %all-gather.5.cloned.1.call-start = ((), (), s32[]{:S(2)}) async-start(), calls=%async_computation.2 | async-start | bytes 1114112 | tf_op jit(solution)/shard_map/while/body/eval_jaxpr/all_gather | solution.py:77
  1207.4 73.8 %all-gather.3.cloned.1.call-start = ((), (), s32[]{:S(2)}) async-start(), calls=%async_computation.1 | async-start | bytes 1114112 | tf_op jit(solution)/shard_map/while/body/eval_jaxpr/all_gather | solution.py:73
  1243.4 103.9 %all-gather.5.cloned.1.call-start = ((), (), s32[]{:S(2)}) async-start(), calls=%async_computation.2 | async-start | bytes 1114112 | tf_op jit(solution)/shard_map/while/body/eval_jaxpr/all_gather | solution.py:77
  1347.4 73.8 %all-gather.3.cloned.1.call-start = ((), (), s32[]{:S(2)}) async-start(), calls=%async_computation.1 | async-start | bytes 1114112 | tf_op jit(solution)/shard_map/while/body/eval_jaxpr/all_gather | solution.py:73
  1383.5 103.9 %all-gather.5.cloned.1.call-start = ((), (), s32[]{:S(2)}) async-start(), calls=%async_computation.2 | async-start | bytes 1114112 | tf_op jit(solution)/shard_map/while/body/eval_jaxpr/all_gather | solution.py:77
  1487.4 73.8 %all-gather.3.cloned.1.call-start = ((), (), s32[]{:S(2)}) async-start(), calls=%async_computation.1 | async-start | bytes 1114112 | tf_op jit(solution)/shard_map/while/body/eval_jaxpr/all_gather | solution.py:73
  1523.5 103.9 %all-gather.5.cloned.1.call-start = ((), (), s32[]{:S(2)}) async-start(), calls=%async_computation.2 | async-start | bytes 1114112 | tf_op jit(solution)/shard_map/while/body/eval_jaxpr/all_gather | solution.py:77
  (25 other events, 2580.7 us)
Sparse Core Ops, SparseCore 0:
  10.5 86.3 all-reduce.1
  120.3 40.5 all-gather.2
  164.4 42.9 all-gather.4
  263.4 37.5 all-gather.2
  304.4 42.9 all-gather.4
  403.4 37.5 all-gather.2
  444.4 42.9 all-gather.4
  543.4 37.5 all-gather.2
  584.5 42.9 all-gather.4
  683.4 37.5 all-gather.2
  724.5 42.9 all-gather.4
  823.5 37.5 all-gather.2
  864.5 42.9 all-gather.4
  963.5 37.5 all-gather.2
  1004.5 42.9 all-gather.4
  1103.5 37.5 all-gather.2
  1144.6 42.9 all-gather.4
  1243.5 37.5 all-gather.2
  1284.6 42.9 all-gather.4
  1383.6 37.5 all-gather.2
  1424.6 42.9 all-gather.4
  1523.6 37.5 all-gather.2
  1564.6 42.9 all-gather.4
where the time goes:
time: 1660 us
  blocking collectives  671 us (40%)
  waiting for transfers between devices  657 us (40%)
  starting transfers between devices  182 us (11%)
  matrix products  95 us (6%)
  other arithmetic  26.3 us (2%)
  local copies, waits for them, and re-layouts  17.8 us (1%)
    psum x11, blocking collectives, tick(): lax.psum(partial_out.reshape(block_rows, -1), 'tp')  643 us
    all_gather x11, waiting for transfers between devices, tick(): lax.all_gather(middle_own, 'tp', axis=1, tiled=True)  417 us
    ppermute x11, starting transfers between devices, from_behind(): return lax.ppermute(value, axis, pairs)  181 us
    ppermute x11, waiting for transfers between devices, from_behind(): return lax.ppermute(value, axis, pairs)  151 us
    psum x1, waiting for transfers between devices, shards(): lax.psum(partial_in.reshape(total_tokens, -1), 'tp')  87.7 us
    dot_general x11, matrix products, contract_columns(): lax.dot_general(portion, matrix, (((1,), (1,)), ((), ())), preferred_elem...  36.4 us
    dot_general x11, matrix products, tick(): lax.dot_general(upper_full, weights[1], (((1,), (1,)), ((), ())), preferr...  33.7 us
  transfers between devices with their start and end apart: 34, of which 23 were waited for; matrix products, arithmetic and copies ran while one was open for 3% of the time, Pallas kernels for 0%

commit v1 on v0

--- a/solution.py
+++ b/solution.py
@@ -7,6 +7,7 @@
 SEQ_MB = 1
 MB = 4
 EXAMPLES = 2
+show_row_in = lambda u: jnp.sum(lax.all_gather(u, axis_name="tp"), axis=0)
 
 
 def from_behind(value, axis, by):
@@ -79,7 +80,7 @@
         partial_out = jnp.einsum(
             "lrd,ldk->rlk", cotangents, output_basis, preferred_element_type=jnp.float32
         )
-        out_feats = lax.psum(partial_out.reshape(block_rows, -1), "tp").reshape(partial_out.shape)
+        out_feats = show_row_in(partial_out.reshape(block_rows, -1)).reshape(partial_out.shape)
         in_block = lax.dynamic_slice_in_dim(in_feats, first_row, block_rows, 0)
         block_examples = jnp.repeat(
             lax.dynamic_slice_in_dim(sequence_example, micro_clip * SEQ_MB, SEQ_MB, 0), SEQLEN

time: 1660 us -> 1330 us (0.80)
  blocking collectives: 671 us -> 223 us
  waiting for transfers between devices: 657 us -> 903 us
  starting transfers between devices: 182 us -> 43.7 us
    psum x11 -> x0, blocking collectives: 643 us -> none  [tick(): lax.psum(partial_out.reshape(block_rows, -1), 'tp')]
    all_gather x11, waiting for transfers between devices: 0.19 us -> 217 us  [tick(): new_outgoing = lax.all_gather(lower_own, 'tp', axis=1, tiled=True)]
    all_gather x0 -> x11, blocking collectives: none -> 208 us  [show_row_in = lambda u: jnp.sum(lax.all_gather(u, axis_name='tp'), axis=0)]
    ppermute x11, starting transfers between devices: 181 us -> 43.2 us  [from_behind(): return lax.ppermute(value, axis, pairs)]
    all_gather x11, waiting for transfers between devices: 417 us -> 447 us  [tick(): lax.all_gather(middle_own, 'tp', axis=1, tiled=True)]
  transfers between devices with their start and end apart: 34 -> 34, of which waited for: 23 -> 34; matrix products, arithmetic and copies ran while one was open for 3% -> 4% of each run, Pallas kernels for 0% -> 0%
where the time goes in v1:
time: 1330 us; the launch traced here: 1320 us
  waiting for transfers between devices  903 us (68%)
  blocking collectives  223 us (17%)
  matrix products  95 us (7%)
  starting transfers between devices  43.7 us (3%)
  other arithmetic  26.7 us (2%)
  local copies, waits for them, and re-layouts  17.8 us (1%)
    all_gather x11, waiting for transfers between devices, tick(): lax.all_gather(middle_own, 'tp', axis=1, tiled=True)  447 us
    all_gather x11, waiting for transfers between devices, tick(): new_outgoing = lax.all_gather(lower_own, 'tp', axis=1, tiled=True)  217 us
    all_gather x11, blocking collectives, show_row_in = lambda u: jnp.sum(lax.all_gather(u, axis_name='tp'), axis=0)  208 us
    ppermute x11, waiting for transfers between devices, from_behind(): return lax.ppermute(value, axis, pairs)  151 us
    psum x1, waiting for transfers between devices, shards(): lax.psum(partial_in.reshape(total_tokens, -1), 'tp')  87.7 us
    ppermute x11, starting transfers between devices, from_behind(): return lax.ppermute(value, axis, pairs)  43.2 us
    dot_general x11, matrix products, contract_columns(): lax.dot_general(portion, matrix, (((1,), (1,)), ((), ())), preferred_elem...  36.4 us
    dot_general x11, matrix products, tick(): lax.dot_general(upper_full, weights[1], (((1,), (1,)), ((), ())), preferr...  33.6 us
  transfers between devices with their start and end apart: 34, of which 34 were waited for; matrix products, arithmetic and copies ran while one was open for 4% of the time, Pallas kernels for 0%

profile of v1, /device:TPU:1, one launch (start us, length us, event | category | flops | bytes accessed | tf_op | source)
XLA Modules:
  0.0 1323.0 jit_solution(3568479040223697870)
XLA Ops:
  9.2 87.7 %all-reduce.2.cloned.1.call-done = f32[512,2,64]{0,2,1:T(8,128)} async-done(((f32[512,2,64]{0,2,1:T(8,128)}), f32[512,2,64]{0,2,1:T(8,128)}) %all-reduce.2.cloned.1.call-update) | async-done | bytes 262160 | tf_op jit(solution)/shard_map/psum | solution.py:50
  98.0 1203.8 %while.18 = (s32[]{:T(128)}, bf16[128,4096]{1,0:T(8,128)(2,1)}, f32[2,2,2048]{2,1,0:T(2,128)S(1)}, pred[]{:T(512)}, s32[]{:T(128)}, /*index=5*/bf16[512,4096]{1,...) while((s32[]{:T(128)}, bf16[128,4096]{1,0:T(8,128)(2,1)}, ...), condition=%wide.region_3.4_spmd.clone, body=%wide.region_1.3_spmd.clone.sunk | while | flops 555163648 | bytes 27034632 | solution.py:102
  120.3 40.6 %all-gather.3.cloned.1.call-done = bf16[128,4096]{1,0:T(8,128)(2,1)} async-done(((bf16[128,256]{1,0:T(8,128)(2,1)}), bf16[128,4096]{1,0:T(8,128)(2,1)}) %all-gather.3.cloned.1.call-update) | async-done | bytes 1048592 | tf_op jit(solution)/shard_map/while/body/eval_jaxpr/all_gather | solution.py:74
  187.7 19.7 %all-gather.5.cloned.1.call-done = bf16[128,4096]{1,0:T(8,128)(2,1)} async-done(((bf16[128,256]{1,0:T(8,128)(2,1)}), bf16[128,4096]{1,0:T(8,128)(2,1)}) %all-gather.5.cloned.1.call-update) | async-done | bytes 1048592 | tf_op jit(solution)/shard_map/while/body/eval_jaxpr/all_gather | solution.py:78
  229.7 40.6 %all-gather.3.cloned.1.call-done = bf16[128,4096]{1,0:T(8,128)(2,1)} async-done(((bf16[128,256]{1,0:T(8,128)(2,1)}), bf16[128,4096]{1,0:T(8,128)(2,1)}) %all-gather.3.cloned.1.call-update) | async-done | bytes 1048592 | tf_op jit(solution)/shard_map/while/body/eval_jaxpr/all_gather | solution.py:74
  297.1 19.7 %all-gather.5.cloned.1.call-done = bf16[128,4096]{1,0:T(8,128)(2,1)} async-done(((bf16[128,256]{1,0:T(8,128)(2,1)}), bf16[128,4096]{1,0:T(8,128)(2,1)}) %all-gather.5.cloned.1.call-update) | async-done | bytes 1048592 | tf_op jit(solution)/shard_map/while/body/eval_jaxpr/all_gather | solution.py:78
  339.1 40.6 %all-gather.3.cloned.1.call-done = bf16[128,4096]{1,0:T(8,128)(2,1)} async-done(((bf16[128,256]{1,0:T(8,128)(2,1)}), bf16[128,4096]{1,0:T(8,128)(2,1)}) %all-gather.3.cloned.1.call-update) | async-done | bytes 1048592 | tf_op jit(solution)/shard_map/while/body/eval_jaxpr/all_gather | solution.py:74
  406.6 19.7 %all-gather.5.cloned.1.call-done = bf16[128,4096]{1,0:T(8,128)(2,1)} async-done(((bf16[128,256]{1,0:T(8,128)(2,1)}), bf16[128,4096]{1,0:T(8,128)(2,1)}) %all-gather.5.cloned.1.call-update) | async-done | bytes 1048592 | tf_op jit(solution)/shard_map/while/body/eval_jaxpr/all_gather | solution.py:78
  448.6 40.6 %all-gather.3.cloned.1.call-done = bf16[128,4096]{1,0:T(8,128)(2,1)} async-done(((bf16[128,256]{1,0:T(8,128)(2,1)}), bf16[128,4096]{1,0:T(8,128)(2,1)}) %all-gather.3.cloned.1.call-update) | async-done | bytes 1048592 | tf_op jit(solution)/shard_map/while/body/eval_jaxpr/all_gather | solution.py:74
  516.0 19.7 %all-gather.5.cloned.1.call-done = bf16[128,4096]{1,0:T(8,128)(2,1)} async-done(((bf16[128,256]{1,0:T(8,128)(2,1)}), bf16[128,4096]{1,0:T(8,128)(2,1)}) %all-gather.5.cloned.1.call-update) | async-done | bytes 1048592 | tf_op jit(solution)/shard_map/while/body/eval_jaxpr/all_gather | solution.py:78
  558.0 40.6 %all-gather.3.cloned.1.call-done = bf16[128,4096]{1,0:T(8,128)(2,1)} async-done(((bf16[128,256]{1,0:T(8,128)(2,1)}), bf16[128,4096]{1,0:T(8,128)(2,1)}) %all-gather.3.cloned.1.call-update) | async-done | bytes 1048592 | tf_op jit(solution)/shard_map/while/body/eval_jaxpr/all_gather | solution.py:74
  625.5 19.7 %all-gather.5.cloned.1.call-done = bf16[128,4096]{1,0:T(8,128)(2,1)} async-done(((bf16[128,256]{1,0:T(8,128)(2,1)}), bf16[128,4096]{1,0:T(8,128)(2,1)}) %all-gather.5.cloned.1.call-update) | async-done | bytes 1048592 | tf_op jit(solution)/shard_map/while/body/eval_jaxpr/all_gather | solution.py:78
  667.5 40.6 %all-gather.3.cloned.1.call-done = bf16[128,4096]{1,0:T(8,128)(2,1)} async-done(((bf16[128,256]{1,0:T(8,128)(2,1)}), bf16[128,4096]{1,0:T(8,128)(2,1)}) %all-gather.3.cloned.1.call-update) | async-done | bytes 1048592 | tf_op jit(solution)/shard_map/while/body/eval_jaxpr/all_gather | solution.py:74
  734.9 19.7 %all-gather.5.cloned.1.call-done = bf16[128,4096]{1,0:T(8,128)(2,1)} async-done(((bf16[128,256]{1,0:T(8,128)(2,1)}), bf16[128,4096]{1,0:T(8,128)(2,1)}) %all-gather.5.cloned.1.call-update) | async-done | bytes 1048592 | tf_op jit(solution)/shard_map/while/body/eval_jaxpr/all_gather | solution.py:78
  776.9 40.6 %all-gather.3.cloned.1.call-done = bf16[128,4096]{1,0:T(8,128)(2,1)} async-done(((bf16[128,256]{1,0:T(8,128)(2,1)}), bf16[128,4096]{1,0:T(8,128)(2,1)}) %all-gather.3.cloned.1.call-update) | async-done | bytes 1048592 | tf_op jit(solution)/shard_map/while/body/eval_jaxpr/all_gather | solution.py:74
  844.3 19.7 %all-gather.5.cloned.1.call-done = bf16[128,4096]{1,0:T(8,128)(2,1)} async-done(((bf16[128,256]{1,0:T(8,128)(2,1)}), bf16[128,4096]{1,0:T(8,128)(2,1)}) %all-gather.5.cloned.1.call-update) | async-done | bytes 1048592 | tf_op jit(solution)/shard_map/while/body/eval_jaxpr/all_gather | solution.py:78
  886.3 40.6 %all-gather.3.cloned.1.call-done = bf16[128,4096]{1,0:T(8,128)(2,1)} async-done(((bf16[128,256]{1,0:T(8,128)(2,1)}), bf16[128,4096]{1,0:T(8,128)(2,1)}) %all-gather.3.cloned.1.call-update) | async-done | bytes 1048592 | tf_op jit(solution)/shard_map/while/body/eval_jaxpr/all_gather | solution.py:74
  953.8 19.7 %all-gather.5.cloned.1.call-done = bf16[128,4096]{1,0:T(8,128)(2,1)} async-done(((bf16[128,256]{1,0:T(8,128)(2,1)}), bf16[128,4096]{1,0:T(8,128)(2,1)}) %all-gather.5.cloned.1.call-update) | async-done | bytes 1048592 | tf_op jit(solution)/shard_map/while/body/eval_jaxpr/all_gather | solution.py:78
  995.8 40.6 %all-gather.3.cloned.1.call-done = bf16[128,4096]{1,0:T(8,128)(2,1)} async-done(((bf16[128,256]{1,0:T(8,128)(2,1)}), bf16[128,4096]{1,0:T(8,128)(2,1)}) %all-gather.3.cloned.1.call-update) | async-done | bytes 1048592 | tf_op jit(solution)/shard_map/while/body/eval_jaxpr/all_gather | solution.py:74
  1063.2 19.7 %all-gather.5.cloned.1.call-done = bf16[128,4096]{1,0:T(8,128)(2,1)} async-done(((bf16[128,256]{1,0:T(8,128)(2,1)}), bf16[128,4096]{1,0:T(8,128)(2,1)}) %all-gather.5.cloned.1.call-update) | async-done | bytes 1048592 | tf_op jit(solution)/shard_map/while/body/eval_jaxpr/all_gather | solution.py:78
  1105.2 40.6 %all-gather.3.cloned.1.call-done = bf16[128,4096]{1,0:T(8,128)(2,1)} async-done(((bf16[128,256]{1,0:T(8,128)(2,1)}), bf16[128,4096]{1,0:T(8,128)(2,1)}) %all-gather.3.cloned.1.call-update) | async-done | bytes 1048592 | tf_op jit(solution)/shard_map/while/body/eval_jaxpr/all_gather | solution.py:74
  1172.7 19.7 %all-gather.5.cloned.1.call-done = bf16[128,4096]{1,0:T(8,128)(2,1)} async-done(((bf16[128,256]{1,0:T(8,128)(2,1)}), bf16[128,4096]{1,0:T(8,128)(2,1)}) %all-gather.5.cloned.1.call-update) | async-done | bytes 1048592 | tf_op jit(solution)/shard_map/while/body/eval_jaxpr/all_gather | solution.py:78
  1214.7 40.6 %all-gather.3.cloned.1.call-done = bf16[128,4096]{1,0:T(8,128)(2,1)} async-done(((bf16[128,256]{1,0:T(8,128)(2,1)}), bf16[128,4096]{1,0:T(8,128)(2,1)}) %all-gather.3.cloned.1.call-update) | async-done | bytes 1048592 | tf_op jit(solution)/shard_map/while/body/eval_jaxpr/all_gather | solution.py:74
  1282.1 19.7 %all-gather.5.cloned.1.call-done = bf16[128,4096]{1,0:T(8,128)(2,1)} async-done(((bf16[128,256]{1,0:T(8,128)(2,1)}), bf16[128,4096]{1,0:T(8,128)(2,1)}) %all-gather.5.cloned.1.call-update) | async-done | bytes 1048592 | tf_op jit(solution)/shard_map/while/body/eval_jaxpr/all_gather | solution.py:78
  (236 shorter events, 557.2 us)
Async XLA Ops:
  6.5 90.4 %all-reduce.2.cloned.1.call-start = ((), (), s32[]{:S(2)}) async-start(), calls=%async_computation | async-start | bytes 524288 | tf_op jit(solution)/shard_map/psum | solution.py:50
  98.0 62.9 %all-gather.3.cloned.1.call-start = ((), (), s32[]{:S(2)}) async-start(), calls=%async_computation.1 | async-start | bytes 1114112 | tf_op jit(solution)/shard_map/while/body/eval_jaxpr/all_gather | solution.py:74
  120.2 87.2 %all-gather.5.cloned.1.call-start = ((), (), s32[]{:S(2)}) async-start(), calls=%async_computation.2 | async-start | bytes 1114112 | tf_op jit(solution)/shard_map/while/body/eval_jaxpr/all_gather | solution.py:78
  207.4 63.0 %all-gather.3.cloned.1.call-start = ((), (), s32[]{:S(2)}) async-start(), calls=%async_computation.1 | async-start | bytes 1114112 | tf_op jit(solution)/shard_map/while/body/eval_jaxpr/all_gather | solution.py:74
  207.4 17.7 %collective-permute-start = (bf16[128,4096]{1,0:T(8,128)(2,1)}, bf16[128,4096]{1,0:T(8,128)(2,1)S(1)}, u32[]{:S(2)}, u32[]{:S(2)}) collective-permute-start(bf16[128,4096]{1,0:T(8,128)(2,1)} %get-tuple-element.466), channel_id=1, source_target_pairs={{16,0},{32,16},{48,32},{64,48},{80,64},{96,80},{112,96},{17,1},{33... | collective-permute-start | bytes 3145736 | tf_op jit(solution)/shard_map/while/body/eval_jaxpr/ppermute | solution.py:16
  229.7 87.2 %all-gather.5.cloned.1.call-start = ((), (), s32[]{:S(2)}) async-start(), calls=%async_computation.2 | async-start | bytes 1114112 | tf_op jit(solution)/shard_map/while/body/eval_jaxpr/all_gather | solution.py:78
  316.8 63.0 %all-gather.3.cloned.1.call-start = ((), (), s32[]{:S(2)}) async-start(), calls=%async_computation.1 | async-start | bytes 1114112 | tf_op jit(solution)/shard_map/while/body/eval_jaxpr/all_gather | solution.py:74
  339.1 87.2 %all-gather.5.cloned.1.call-start = ((), (), s32[]{:S(2)}) async-start(), calls=%async_computation.2 | async-start | bytes 1114112 | tf_op jit(solution)/shard_map/while/body/eval_jaxpr/all_gather | solution.py:78
  426.3 63.0 %all-gather.3.cloned.1.call-start = ((), (), s32[]{:S(2)}) async-start(), calls=%async_computation.1 | async-start | bytes 1114112 | tf_op jit(solution)/shard_map/while/body/eval_jaxpr/all_gather | solution.py:74
  448.5 87.2 %all-gather.5.cloned.1.call-start = ((), (), s32[]{:S(2)}) async-start(), calls=%async_computation.2 | async-start | bytes 1114112 | tf_op jit(solution)/shard_map/while/body/eval_jaxpr/all_gather | solution.py:78
  535.7 63.0 %all-gather.3.cloned.1.call-start = ((), (), s32[]{:S(2)}) async-start(), calls=%async_computation.1 | async-start | bytes 1114112 | tf_op jit(solution)/shard_map/while/body/eval_jaxpr/all_gather | solution.py:74
  558.0 87.2 %all-gather.5.cloned.1.call-start = ((), (), s32[]{:S(2)}) async-start(), calls=%async_computation.2 | async-start | bytes 1114112 | tf_op jit(solution)/shard_map/while/body/eval_jaxpr/all_gather | solution.py:78
  645.2 63.0 %all-gather.3.cloned.1.call-start = ((), (), s32[]{:S(2)}) async-start(), calls=%async_computation.1 | async-start | bytes 1114112 | tf_op jit(solution)/shard_map/while/body/eval_jaxpr/all_gather | solution.py:74
  667.4 87.2 %all-gather.5.cloned.1.call-start = ((), (), s32[]{:S(2)}) async-start(), calls=%async_computation.2 | async-start | bytes 1114112 | tf_op jit(solution)/shard_map/while/body/eval_jaxpr/all_gather | solution.py:78
  754.6 63.0 %all-gather.3.cloned.1.call-start = ((), (), s32[]{:S(2)}) async-start(), calls=%async_computation.1 | async-start | bytes 1114112 | tf_op jit(solution)/shard_map/while/body/eval_jaxpr/all_gather | solution.py:74
  776.9 87.2 %all-gather.5.cloned.1.call-start = ((), (), s32[]{:S(2)}) async-start(), calls=%async_computation.2 | async-start | bytes 1114112 | tf_op jit(solution)/shard_map/while/body/eval_jaxpr/all_gather | solution.py:78
  864.0 63.0 %all-gather.3.cloned.1.call-start = ((), (), s32[]{:S(2)}) async-start(), calls=%async_computation.1 | async-start | bytes 1114112 | tf_op jit(solution)/shard_map/while/body/eval_jaxpr/all_gather | solution.py:74
  886.3 87.2 %all-gather.5.cloned.1.call-start = ((), (), s32[]{:S(2)}) async-start(), calls=%async_computation.2 | async-start | bytes 1114112 | tf_op jit(solution)/shard_map/while/body/eval_jaxpr/all_gather | solution.py:78
  973.5 63.0 %all-gather.3.cloned.1.call-start = ((), (), s32[]{:S(2)}) async-start(), calls=%async_computation.1 | async-start | bytes 1114112 | tf_op jit(solution)/shard_map/while/body/eval_jaxpr/all_gather | solution.py:74
  995.7 87.2 %all-gather.5.cloned.1.call-start = ((), (), s32[]{:S(2)}) async-start(), calls=%async_computation.2 | async-start | bytes 1114112 | tf_op jit(solution)/shard_map/while/body/eval_jaxpr/all_gather | solution.py:78
  1082.9 63.0 %all-gather.3.cloned.1.call-start = ((), (), s32[]{:S(2)}) async-start(), calls=%async_computation.1 | async-start | bytes 1114112 | tf_op jit(solution)/shard_map/while/body/eval_jaxpr/all_gather | solution.py:74
  1105.2 87.2 %all-gather.5.cloned.1.call-start = ((), (), s32[]{:S(2)}) async-start(), calls=%async_computation.2 | async-start | bytes 1114112 | tf_op jit(solution)/shard_map/while/body/eval_jaxpr/all_gather | solution.py:78
  1192.4 63.0 %all-gather.3.cloned.1.call-start = ((), (), s32[]{:S(2)}) async-start(), calls=%async_computation.1 | async-start | bytes 1114112 | tf_op jit(solution)/shard_map/while/body/eval_jaxpr/all_gather | solution.py:74
  1214.6 87.2 %all-gather.5.cloned.1.call-start = ((), (), s32[]{:S(2)}) async-start(), calls=%async_computation.2 | async-start | bytes 1114112 | tf_op jit(solution)/shard_map/while/body/eval_jaxpr/all_gather | solution.py:78
  (25 other events, 2161.4 us)
Sparse Core Ops, SparseCore 0:
  10.5 86.3 all-reduce.1
  120.3 40.5 all-gather.2
  164.4 42.9 all-gather.4
  229.8 40.5 all-gather.2
  273.8 42.9 all-gather.4
  339.2 40.5 all-gather.2
  383.3 42.9 all-gather.4
  448.6 40.5 all-gather.2
  492.7 42.9 all-gather.4
  558.1 40.5 all-gather.2
  602.1 42.9 all-gather.4
  667.5 40.5 all-gather.2
  711.6 42.9 all-gather.4
  777.0 40.5 all-gather.2
  821.0 42.9 all-gather.4
  886.4 40.5 all-gather.2
  930.5 42.9 all-gather.4
  995.8 40.5 all-gather.2
  1039.9 42.9 all-gather.4
  1105.3 40.5 all-gather.2
  1149.3 42.9 all-gather.4
  1214.7 40.5 all-gather.2
  1258.8 42.9 all-gather.4
